TPU v7x, 32 devices: a whole 2x2x4 slice. The times are simulated.
32 devices in a mesh: rows: 8 (over z, y), modes: 4 (over x, core).
Axes of the slice: x: 2, y: 2, z: 4, core: 2. Of those that a mesh axis runs over, the one named last changes fastest.
Arguments:
- mode_slab: bfloat16 [4096, 512], P('rows', 'modes'), may hold values from -25 to 25
- mass_diag: float32 [4096], P('rows'), may hold values from 9.5 to 19
- mass_gain: float32 [4096], P('rows'), may hold values from 0.5 to 1.5
- band_coef: float32 [4], replicated, may hold values from 0.2 to 0.5
- band_offsets: int32 [4], replicated, may hold values from 1 to 64, as said below
- boundary_blocks: int32 [16, 4], P('rows'), may hold values from 0 to 31, as said below
- boundary_counts: int32 [16], P('rows'), may hold values from 2 to 4, as said below
- boundary_modes: bfloat16 [16, 512, 512], P('rows'), may hold values from -0.5 to 0.5
Outputs:
- projected: bfloat16 [16, 512, 512], P('rows', 'modes')
Inputs may be any that keep to these rules, and one draw needn't show every extreme that they name: `band_offsets`: the offsets are distinct and one of them equals 64. `boundary_blocks`: entries of one component are distinct. For component c with e = c // 2, every entry b (used or not) satisfies (b - e * 4 + 512 // 256) mod (32) < 8. Among the used entries of the components of each index e of rows, one is the block just below e's rows and one the block just above them, counted cyclically. `boundary_counts`: some component uses all 4 blocks.
All inputs are finite; a program needn't handle non-finite values.
Results may differ from a plain program's by a relative error of at most 0.0035.
The roundings to bfloat16 on the way count: a program that leaves them out, or rounds other values in their place, can miss the bound.
Values may be sent and summed in bfloat16 or wider, within the bound.
No kernel may reach another device: no remote copies, remote signals or barrier semaphores. Data moves between devices by JAX's collectives and lax.ppermute only.
A program may use at most 64 MiB of HBM per device.

v0:
```python
import jax
import jax.numpy as jnp
from jax import lax
from jax.sharding import PartitionSpec as P

CB = 512
BLOCK = 128
BMAX = 4
NOFF = 4
BAND = 64


def padded_2(block, sides, width, periodic):
    for axis, dim in sides:
        count = lax.axis_size(axis)
        forward = [(i, i + 1) for i in range(count - 1)]
        if periodic:
            forward.append((count - 1, 0))
        backward = [(target, source) for source, target in forward]
        low = lax.ppermute(
            lax.slice_in_dim(block, block.shape[dim] - width, None, axis=dim), axis, forward
        )
        high = lax.ppermute(lax.slice_in_dim(block, 0, width, axis=dim), axis, backward)
        block = jnp.concatenate([low, block, high], axis=dim)
    return block


def local(
    mode_slab,
    mass_diag,
    mass_gain,
    band_coef,
    band_offsets,
    boundary_blocks,
    boundary_counts,
    boundary_modes,
):
    rows_dev, mode_cols = mode_slab.shape
    per_dev = rows_dev // BLOCK
    rim_rows = per_dev // 2 * BLOCK
    slab_float = mode_slab.astype(jnp.float32)
    scaled = (mass_gain[:, None] * slab_float).astype(jnp.bfloat16)
    padded = padded_2(scaled, (("rows", 0),), BAND, False)
    neighbour = jnp.zeros((rows_dev, mode_cols), jnp.float32)
    for j in range(NOFF):
        offset = band_offsets[j]
        upward = lax.dynamic_slice_in_dim(padded, BAND + offset, rows_dev, 0)
        downward = lax.dynamic_slice_in_dim(padded, BAND - offset, rows_dev, 0)
        neighbour = neighbour + band_coef[j] * (
            upward.astype(jnp.float32) + downward.astype(jnp.float32)
        )
    mass_image = (mass_diag[:, None] * slab_float + mass_gain[:, None] * neighbour).astype(
        jnp.bfloat16
    )
    every_mode = lax.all_gather(mass_image, "modes", axis=1, tiled=True)
    full_order = every_mode.shape[1]
    total_rows = rows_dev * lax.axis_size("rows")
    partial_value = (
        lax.dot_general(
            every_mode, mode_slab, (((0,), (0,)), ((), ())), preferred_element_type=jnp.float32
        )
        / total_rows
    )
    column_block = lax.psum(partial_value, "rows")
    gram_matrix = lax.all_gather(column_block, "modes", axis=1, tiled=True)
    lower_factor = jnp.linalg.cholesky(gram_matrix)
    first_column = lax.axis_index("modes") * mode_cols
    unit_columns = (
        lax.broadcasted_iota(jnp.int32, (full_order, mode_cols), 0)
        == lax.broadcasted_iota(jnp.int32, (full_order, mode_cols), 1) + first_column
    ).astype(jnp.float32)
    inverse = jax.scipy.linalg.solve_triangular(
        lower_factor, unit_columns, lower=True, trans=1
    ).astype(jnp.bfloat16)
    mass_basis = jnp.dot(every_mode, inverse, preferred_element_type=jnp.float32).astype(
        jnp.bfloat16
    )
    extended = padded_2(mass_basis, (("rows", 0),), rim_rows, True)
    total_blocks = per_dev * lax.axis_size("rows")
    window_start = lax.axis_index("rows") * per_dev - per_dev // 2
    local_blocks = jnp.mod(boundary_blocks - window_start, total_blocks)
    owned = boundary_modes.shape[0]
    shaped = boundary_modes.reshape(owned, BMAX, BLOCK, CB)
    row_index = local_blocks[:, :, None] * BLOCK + jnp.arange(BLOCK, dtype=jnp.int32)[None, None, :]
    picked = jnp.take(extended, row_index, axis=0)
    in_use = jnp.arange(BMAX, dtype=jnp.int32)[None, :] < boundary_counts[:, None]
    picked = jnp.where(in_use[:, :, None, None], picked, jnp.zeros_like(picked))
    result = jnp.einsum("csbk,csbm->ckm", picked, shaped, preferred_element_type=jnp.float32)
    return result.astype(jnp.bfloat16)


def solution(mesh):
    in_specs = (
        P("rows", "modes"),
        P("rows"),
        P("rows"),
        P(),
        P(),
        P("rows", None),
        P("rows"),
        P("rows", None, None),
    )
    out_specs = P("rows", "modes", None)
    return jax.shard_map(local, mesh=mesh, in_specs=in_specs, out_specs=out_specs, check_vma=False)
```

profile of v0, /device:TPU:0, one launch (start us, length us, event | category | flops | bytes accessed | tf_op | source)
XLA Modules:
  0.0 294.4 jit_solution(5894387732189599143)
XLA Ops:
  6.5 1.1 fusion.4
  7.7 4.9 %collective-permute-start = (bf16[64,128]{1,0:T(8,128)(2,1)S(1)}, bf16[64,128]{1,0:T(8,128)(2,1)S(1)}, u32[]{:S(2)}, u32[]{:S(2)}) collective-permute-start(bf16[64,128]{1,0:T(8,128)(2,1)S(1)} %get-tuple-element.25), channel_id=1, source_target_pairs={{0,4},{4,8},{8,12},{12,16},{16,20},{20,24},{24,28},{1,5},{5,9},{9,... | collective-permute-start | bytes 49160 | tf_op jit(solution)/shard_map/ppermute | solution.py:20
  12.6 1.3 collective-permute-start.1
  13.9 0.7 fusion.59
  14.6 0.6 fusion.58
  25.6 0.8 copy-done.6
  26.4 2.8 fusion.3
  29.2 7.2 %all_gather.6 = bf16[512,512]{1,0:T(8,128)(2,1)S(1)} all-gather(bf16[512,128]{1,0:T(8,128)(2,1)S(1)} %fusion.3), channel_id=1, replica_groups=mesh['rows'=8,'modes'=4] {'modes'}, dimensions={1}, use_global_device_ids=true | all-gather | bytes 655360 | tf_op jit(solution)/shard_map/all_gather | solution.py:55
  36.4 0.8 copy-done.4
  37.3 1.0 convolution_multiply_fusion
  38.3 72.4 %all-reduce.3.cloned.1.call-done = f32[512,128]{0,1:T(8,128)} async-done(((f32[512,128]{0,1:T(8,128)}), f32[512,128]{0,1:T(8,128)}) %all-reduce.3.cloned.1.call-update) | async-done | bytes 262160 | tf_op jit(solution)/shard_map/psum | solution.py:64
  110.7 0.6 iota_multiply_fusion
  111.3 0.7 copy-done.12
  112.1 0.7 fusion.44
  112.8 15.5 %all-gather.2.cloned.1.call-done = f32[512,512]{0,1:T(8,128)} async-done(((f32[512,128]{0,1:T(8,128)}), f32[512,512]{0,1:T(8,128)}) %all-gather.2.cloned.1.call-update) | async-done | bytes 1048592 | tf_op jit(solution)/shard_map/all_gather | solution.py:65
  128.4 1.6 copy.13
  130.0 0.2 fusion.1
  130.3 1.0 copy-done.2
  131.3 11.7 %cholesky.104 = f32[128,128]{1,0:T(8,128)S(1)} custom-call(f32[128,128]{1,0:T(8,128)S(1)} %cholesky.266), custom_call_target="Cholesky" | custom-call | tf_op jit(solution)/shard_map/jit(cholesky)/cholesky | solution.py:66
  143.1 9.8 %custom-call.31 = f32[1,128,128]{1,2,0:T(8,128)S(1)} custom-call(f32[1,128,128]{2,1,0:T(8,128)S(1)} %get-tuple-element.36), custom_call_target="InvertDiagBlocksLowerTriangular" | custom-call | tf_op jit(solution)/shard_map/jit(cholesky)/cholesky | solution.py:66
  153.0 0.3 constant_dynamic-update-slice_fusion
  153.3 0.3 convolution_subtract_fusion
  153.6 0.7 copy-done.7
  154.3 11.7 %cholesky.217 = f32[128,128]{1,0:T(8,128)S(1)} custom-call(f32[128,128]{1,0:T(8,128)S(1)} %cholesky.270), custom_call_target="Cholesky" | custom-call | tf_op jit(solution)/shard_map/jit(cholesky)/cholesky | solution.py:66
  166.1 9.9 %custom-call.32 = f32[1,128,128]{1,2,0:T(8,128)S(1)} custom-call(f32[1,128,128]{2,1,0:T(8,128)S(1)} %get-tuple-element.33), custom_call_target="InvertDiagBlocksLowerTriangular" | custom-call | tf_op jit(solution)/shard_map/jit(cholesky)/cholesky | solution.py:66
  176.0 1.2 convolution_dynamic-update-slice_fusion
  177.2 0.4 convolution_subtract_fusion.1
  177.6 0.6 cholesky.275
  178.2 13.2 %cholesky.238 = f32[128,128]{1,0:T(8,128)} custom-call(f32[128,128]{1,0:T(8,128)} %cholesky.275), custom_call_target="Cholesky" | custom-call | tf_op jit(solution)/shard_map/jit(cholesky)/cholesky | solution.py:66
  191.4 1.5 select_reduce_fusion.1
  192.9 0.7 compare_reduce_fusion.1
  193.6 11.3 %custom-call.33 = f32[1,128,128]{1,2,0:T(8,128)} custom-call(f32[1,128,128]{2,1,0:T(8,128)} %get-tuple-element.30), custom_call_target="InvertDiagBlocksLowerTriangular" | custom-call | tf_op jit(solution)/shard_map/jit(cholesky)/cholesky | solution.py:66
  204.8 1.0 convolution_dynamic-update-slice_fusion.1
  205.9 0.4 convolution_subtract_fusion.5
  206.3 11.7 %cholesky.255 = f32[128,128]{1,0:T(8,128)S(1)} custom-call(f32[128,128]{1,0:T(8,128)S(1)} %convolution_subtract_fusion.5), custom_call_target="Cholesky" | custom-call | tf_op jit(solution)/shard_map/jit(cholesky)/cholesky | solution.py:66
  218.0 0.3 select_reduce_fusion
  218.2 0.7 compare_reduce_fusion
  218.9 0.7 compare_reduce_fusion.2
  222.1 0.1 select_select_fusion
  222.3 0.5 copy-done.14
  222.8 9.9 %while.1 = (s32[]{:T(128)}, f32[512,512]{1,0:T(8,128)S(1)}, s32[4,2]{0,1:T(2,128)S(1)}, f32[4,128,128]{2,1,0:T(8,128)}, s32[]{:T(128)}) while((s32[]{:T(128)}, f32[512,512]{1,0:T(8,128)S(1)}, s32[4,2]{0,1:T(2,128)S(1)}, f32[4,128,128]{2,1,0:T(8,128)}, s32[]{:T(128)}) %tuple.39), condition=%wide.while_cond, body=%wide.while_body.sunk | while | flops 2 | bytes 132705 | solution.py:72
  222.8 0.5 fusion.73
  223.4 1.9 bitcast_dynamic-update-slice_fusion.2
  225.3 0.5 fusion.73
  225.8 1.9 bitcast_dynamic-update-slice_fusion.2
  227.8 0.5 fusion.73
  228.3 1.9 bitcast_dynamic-update-slice_fusion.2
  230.2 0.5 fusion.73
  230.8 1.9 bitcast_dynamic-update-slice_fusion.2
  232.6 40.1 %custom-call.34 = f32[4,128,128]{1,2,0:T(8,128)S(1)} custom-call(f32[4,128,128]{2,1,0:T(8,128)} %get-tuple-element.12), custom_call_target="InvertDiagBlocksLowerTriangular" | custom-call | tf_op jit(solution)/shard_map/jit(_solve_triangular)/triangular_solve | solution.py:72
  272.8 0.9 fusion.60
  273.6 0.3 convolution_subtract_fusion.3
  273.9 0.2 fusion.61
  274.2 0.4 convolution_subtract_fusion.2
  274.6 0.2 fusion.62
  274.8 0.5 convolution_subtract_fusion.4
  275.3 0.2 convolution_convert_fusion.1
  275.6 0.3 convolution_convert_fusion
  275.9 1.5 collective-permute-start.2
  277.4 3.3 %collective-permute-start.3 = (bf16[256,128]{1,0:T(8,128)(2,1)S(1)}, bf16[256,128]{1,0:T(8,128)(2,1)S(1)}, u32[]{:S(2)}, u32[]{:S(2)}) collective-permute-start(bf16[256,128]{1,0:T(8,128)(2,1)S(1)} %get-tuple-element.24), channel_id=1, source_target_pairs={{4,0},{8,4},{12,8},{16,12},{20,16},{24,20},{28,24},{0,28},{5,1},{9... | collective-permute-start | bytes 196616 | tf_op jit(solution)/shard_map/ppermute | solution.py:23
  280.8 2.2 collective-permute-done.2
  283.1 3.2 %gather_fusion = bf16[1024,128]{1,0:T(8,128)(2,1)S(1)} fusion(bf16[1024,128]{1,0:T(8,128)(2,1)S(1)} %pad_maximum_fusion, s32[1024]{0:T(1024)S(1)} %broadcast_clamp_fusion), kind=kCustom, calls=%fused_computation | custom fusion | bytes 528384 | tf_op jit(solution)/shard_map/jit(_take)/gather | solution.py:85
  286.3 0.2 copy.14
  286.5 1.1 fusion
  (52 shorter events, 1.1 us)
Async XLA Ops:
  6.5 280.0 %copy-start = (bf16[2,512,512]{2,1,0:T(8,128)(2,1)S(1)}, bf16[2,512,512]{2,1,0:T(8,128)(2,1)}, u32[]{:S(2)}) copy-start(bf16[2,512,512]{2,1,0:T(8,128)(2,1)} %param.15) | copy-start | bytes 3145732
  6.5 104.1 %all-reduce.3.cloned.1.call-start = ((), (), s32[]{:S(2)}) async-start(), calls=%async_computation | async-start | bytes 524288 | tf_op jit(solution)/shard_map/psum | solution.py:64
  7.7 6.2 %copy-start.9 = (s32[4]{0:T(128)S(1)}, s32[4]{0:T(128)}, u32[]{:S(2)}) copy-start(s32[4]{0:T(128)} %param.12) | copy-start | bytes 52
  7.7 17.8 %collective-permute-start = (bf16[64,128]{1,0:T(8,128)(2,1)S(1)}, bf16[64,128]{1,0:T(8,128)(2,1)S(1)}, u32[]{:S(2)}, u32[]{:S(2)}) collective-permute-start(bf16[64,128]{1,0:T(8,128)(2,1)S(1)} %get-tuple-element.25), channel_id=1, source_target_pairs={{0,4},{4,8},{8,12},{12,16},{16,20},{20,24},{24,28},{1,5},{5,9},{9,... | collective-permute-start | bytes 49160 | tf_op jit(solution)/shard_map/ppermute | solution.py:20
  12.6 12.9 %collective-permute-start.1 = (bf16[64,128]{1,0:T(8,128)(2,1)S(1)}, bf16[64,128]{1,0:T(8,128)(2,1)S(1)}, u32[]{:S(2)}, u32[]{:S(2)}) collective-permute-start(bf16[64,128]{1,0:T(8,128)(2,1)S(1)} %get-tuple-element.26), channel_id=1, source_target_pairs={{4,0},{8,4},{12,8},{16,12},{20,16},{24,20},{28,24},{5,1},{9,5},{13... | collective-permute-start | bytes 49160 | tf_op jit(solution)/shard_map/ppermute | solution.py:23
  13.9 0.7 copy-start.10
  25.5 0.9 copy-start.6
  25.6 0.9 copy-start.11
  25.6 0.8 copy-start.8
  36.4 0.8 copy-start.4
  38.3 90.1 %all-gather.2.cloned.1.call-start = ((), (), s32[]{:S(2)}) async-start(), calls=%async_computation.1 | async-start | bytes 1310720 | tf_op jit(solution)/shard_map/all_gather | solution.py:65
  111.3 0.7 copy-start.12
  128.4 1.7 copy-start.1
  130.2 1.0 copy-start.2
  131.2 21.7 %copy-start.3 = (f32[512,512]{1,0:T(8,128)S(1)}, f32[512,512]{1,0:T(8,128)}, u32[]{:S(2)}) copy-start(f32[512,512]{1,0:T(8,128)} %copy-done.2) | copy-start | bytes 3145732
  153.6 0.7 copy-start.7
  222.1 0.7 copy-start.14
  274.5 1.0 copy-start.5
  275.9 4.8 %copy-start.13 = (s32[2]{0:T(128)S(1)}, s32[2]{0:T(128)}, u32[]{:S(2)}) copy-start(s32[2]{0:T(128)} %param.14) | copy-start | bytes 28
  275.9 7.1 %collective-permute-start.2 = (bf16[256,128]{1,0:T(8,128)(2,1)S(1)}, bf16[256,128]{1,0:T(8,128)(2,1)S(1)}, u32[]{:S(2)}, u32[]{:S(2)}) collective-permute-start(bf16[256,128]{1,0:T(8,128)(2,1)S(1)} %get-tuple-element.23), channel_id=1, source_target_pairs={{0,4},{4,8},{8,12},{12,16},{16,20},{20,24},{24,28},{28,0},{1,5},{5... | collective-permute-start | bytes 196616 | tf_op jit(solution)/shard_map/ppermute | solution.py:20
  277.4 5.7 %collective-permute-start.3 = (bf16[256,128]{1,0:T(8,128)(2,1)S(1)}, bf16[256,128]{1,0:T(8,128)(2,1)S(1)}, u32[]{:S(2)}, u32[]{:S(2)}) collective-permute-start(bf16[256,128]{1,0:T(8,128)(2,1)S(1)} %get-tuple-element.24), channel_id=1, source_target_pairs={{4,0},{8,4},{12,8},{16,12},{20,16},{24,20},{28,24},{0,28},{5,1},{9... | collective-permute-start | bytes 196616 | tf_op jit(solution)/shard_map/ppermute | solution.py:23
Sparse Core Ops, SparseCore 0:
  38.4 72.2 all-reduce.2
  112.3 15.9 all-gather.1
where the time goes:
time: 295 us; the launch traced here: 294 us
  other arithmetic  129 us (44%)
  waiting for transfers between devices  90.3 us (31%)
  between operations  26.6 us (9%)
  local copies, waits for them, and re-layouts  21.7 us (7%)
  starting transfers between devices  11 us (4%)
  matrix products  8.59 us (3%)
  blocking collectives  7.2 us (2%)
    another operation x14, other arithmetic, local(): lower_factor = jnp.linalg.cholesky(gram_matrix)  83.2 us
    psum x1, waiting for transfers between devices, local(): column_block = lax.psum(partial_value, 'rows')  72.4 us
    another operation x3, other arithmetic, local(): jax.scipy.linalg.solve_triangular(lower_factor, unit_columns, lower=True,...  40.8 us
    all_gather x1, waiting for transfers between devices, local(): gram_matrix = lax.all_gather(column_block, 'modes', axis=1, tiled=True)  15.5 us
    another operation x12, local copies, waits for them, and re-layouts  9.85 us
    all_gather x1, blocking collectives, local(): every_mode = lax.all_gather(mass_image, 'modes', axis=1, tiled=True)  7.2 us
    ppermute x2, starting transfers between devices, padded_2(): lax.ppermute(lax.slice_in_dim(block, block.shape[dim] - width, None, axis...  6.39 us
  transfers between devices with their start and end apart: 6, of which 4 were waited for; matrix products, arithmetic and copies ran while one was open for 1% of the time, Pallas kernels for 0%

commit v1 on v0

--- a/solution.py
+++ b/solution.py
@@ -61,7 +61,8 @@
         )
         / total_rows
     )
-    column_block = lax.psum(partial_value, "rows")
+    blocks = lax.all_gather(partial_value, "rows")
+    column_block = jnp.sum(blocks, axis=0)
     gram_matrix = lax.all_gather(column_block, "modes", axis=1, tiled=True)
     lower_factor = jnp.linalg.cholesky(gram_matrix)
     first_column = lax.axis_index("modes") * mode_cols

time: 295 us -> 271 us (0.919)
  waiting for transfers between devices: 90.3 us -> 68.6 us
  other arithmetic: 129 us -> 126 us
    psum x1 -> x0, waiting for transfers between devices: 72.4 us -> none  [local(): column_block = lax.psum(partial_value, 'rows')]
    all_gather x0 -> x1, waiting for transfers between devices: none -> 51.1 us  [local(): blocks = lax.all_gather(partial_value, 'rows')]
    another operation x14, other arithmetic: 83.2 us -> 78.7 us  [local(): lower_factor = jnp.linalg.cholesky(gram_matrix)]
where the time goes in v1:
time: 271 us; the launch traced here: 270 us
  other arithmetic  126 us (46%)
  waiting for transfers between devices  68.6 us (25%)
  between operations  25.9 us (10%)
  local copies, waits for them, and re-layouts  21.1 us (8%)
  starting transfers between devices  11 us (4%)
  matrix products  9.82 us (4%)
  blocking collectives  7.2 us (3%)
    another operation x14, other arithmetic, local(): lower_factor = jnp.linalg.cholesky(gram_matrix)  78.7 us
    all_gather x1, waiting for transfers between devices, local(): blocks = lax.all_gather(partial_value, 'rows')  51.1 us
    another operation x3, other arithmetic, local(): jax.scipy.linalg.solve_triangular(lower_factor, unit_columns, lower=True,...  40.3 us
    all_gather x1, waiting for transfers between devices, local(): gram_matrix = lax.all_gather(column_block, 'modes', axis=1, tiled=True)  15.1 us
    another operation x12, local copies, waits for them, and re-layouts  10.4 us
    all_gather x1, blocking collectives, local(): every_mode = lax.all_gather(mass_image, 'modes', axis=1, tiled=True)  7.2 us
    ppermute x2, starting transfers between devices, padded_2(): lax.ppermute(lax.slice_in_dim(block, block.shape[dim] - width, None, axis...  6.4 us
    another operation x6, matrix products, local(): lower_factor = jnp.linalg.cholesky(gram_matrix)  5.46 us
  transfers between devices with their start and end apart: 6, of which 4 were waited for; matrix products, arithmetic and copies ran while one was open for 1% of the time, Pallas kernels for 0%

profile of v1, /device:TPU:0, one launch (start us, length us, event | category | flops | bytes accessed | tf_op | source)
XLA Modules:
  0.0 269.8 jit_solution(7855664000502833058)
XLA Ops:
  6.5 1.1 fusion.4
  7.7 4.9 %collective-permute-start = (bf16[64,128]{1,0:T(8,128)(2,1)S(1)}, bf16[64,128]{1,0:T(8,128)(2,1)S(1)}, u32[]{:S(2)}, u32[]{:S(2)}) collective-permute-start(bf16[64,128]{1,0:T(8,128)(2,1)S(1)} %get-tuple-element.25), channel_id=1, source_target_pairs={{0,4},{4,8},{8,12},{12,16},{16,20},{20,24},{24,28},{1,5},{5,9},{9,... | collective-permute-start | bytes 49160 | tf_op jit(solution)/shard_map/ppermute | solution.py:20
  12.6 1.3 collective-permute-start.1
  13.9 1.5 fusion.59
  15.3 1.5 fusion.58
  26.4 3.8 %fusion.3 = bf16[512,128]{1,0:T(8,128)(2,1)S(1)} fusion(bf16[512,128]{1,0:T(8,128)(2,1)} %param.8, bf16[640,128]{1,0:T(8,128)(2,1)S(1)} %pad_maximum_fusion.1, s32[]{:T(128)S(6)} %select_n.68, s32[]{:T(128)S(6)} %select_n.67, f32[]{:T(128)} %bitcast.15, s32[]{:T(128)S(6)} %select_n.66, s32[]{:T(128)S(6)} %select_n.65, f32[]{:T(128)} %bitcast.10, ...), kind=kLoop, calls=%fused_computation.23 | loop fusion | flops 1572864 | bytes 1314864 | tf_op jit(solution)/shard_map/convert_element_type | solution.py:52
  30.2 7.2 %all_gather.12 = bf16[512,512]{1,0:T(8,128)(2,1)S(1)} all-gather(bf16[512,128]{1,0:T(8,128)(2,1)S(1)} %fusion.3), channel_id=1, replica_groups=mesh['rows'=8,'modes'=4] {'modes'}, dimensions={1}, use_global_device_ids=true | all-gather | bytes 655360 | tf_op jit(solution)/shard_map/all_gather | solution.py:55
  37.4 0.8 copy-done.3
  38.2 1.0 convolution_multiply_fusion
  39.3 51.1 %all-gather.6.cloned.1.call-done = f32[4096,128]{1,0:T(8,128)} async-done(((f32[512,128]{1,0:T(8,128)}), f32[4096,128]{1,0:T(8,128)}) %all-gather.6.cloned.1.call-update) | async-done | bytes 2097168 | tf_op jit(solution)/shard_map/all_gather | solution.py:64
  90.4 1.7 reduce_sum.9
  92.2 0.8 copy.13
  93.1 0.1 fusion.47
  93.2 0.1 compare_select_fusion
  93.3 15.1 %all-gather.4.cloned.1.call-done = f32[512,512]{0,1:T(8,128)} async-done(((f32[512,128]{0,1:T(8,128)}), f32[512,512]{0,1:T(8,128)}) %all-gather.4.cloned.1.call-update) | async-done | bytes 1048592 | tf_op jit(solution)/shard_map/all_gather | solution.py:66
  108.4 1.6 copy.14
  110.1 0.2 fusion.1
  110.3 1.0 copy-done.2
  111.3 11.7 %cholesky.104 = f32[128,128]{1,0:T(8,128)S(1)} custom-call(f32[128,128]{1,0:T(8,128)S(1)} %cholesky.266), custom_call_target="Cholesky" | custom-call | tf_op jit(solution)/shard_map/jit(cholesky)/cholesky | solution.py:67
  123.0 0.1 cholesky.224
  123.1 9.8 %custom-call.31 = f32[1,128,128]{1,2,0:T(8,128)S(1)} custom-call(f32[1,128,128]{2,1,0:T(8,128)S(1)} %get-tuple-element.36), custom_call_target="InvertDiagBlocksLowerTriangular" | custom-call | tf_op jit(solution)/shard_map/jit(cholesky)/cholesky | solution.py:67
  133.0 1.2 constant_dynamic-update-slice_fusion
  134.2 1.3 convolution_subtract_fusion
  135.5 11.7 %cholesky.217 = f32[128,128]{1,0:T(8,128)S(1)} custom-call(f32[128,128]{1,0:T(8,128)S(1)} %cholesky.270), custom_call_target="Cholesky" | custom-call | tf_op jit(solution)/shard_map/jit(cholesky)/cholesky | solution.py:67
  147.2 10.0 %custom-call.32 = f32[1,128,128]{1,2,0:T(8,128)S(1)} custom-call(f32[1,128,128]{2,1,0:T(8,128)S(1)} %get-tuple-element.33), custom_call_target="InvertDiagBlocksLowerTriangular" | custom-call | tf_op jit(solution)/shard_map/jit(cholesky)/cholesky | solution.py:67
  157.2 0.3 convolution_dynamic-update-slice_fusion
  157.5 1.3 convolution_subtract_fusion.1
  158.8 11.7 %cholesky.238 = f32[128,128]{1,0:T(8,128)S(1)} custom-call(f32[128,128]{1,0:T(8,128)S(1)} %cholesky.275), custom_call_target="Cholesky" | custom-call | tf_op jit(solution)/shard_map/jit(cholesky)/cholesky | solution.py:67
  170.5 0.7 compare_reduce_fusion.1
  171.2 9.8 %custom-call.33 = f32[1,128,128]{1,2,0:T(8,128)S(1)} custom-call(f32[1,128,128]{2,1,0:T(8,128)S(1)} %get-tuple-element.30), custom_call_target="InvertDiagBlocksLowerTriangular" | custom-call | tf_op jit(solution)/shard_map/jit(cholesky)/cholesky | solution.py:67
  181.0 0.2 convolution_dynamic-update-slice_fusion.1
  181.2 1.2 convolution_subtract_fusion.5
  182.4 11.9 %cholesky.255 = f32[128,128]{1,0:T(8,128)S(1)} custom-call(f32[128,128]{1,0:T(8,128)S(1)} %convolution_subtract_fusion.5), custom_call_target="Cholesky" | custom-call | tf_op jit(solution)/shard_map/jit(cholesky)/cholesky | solution.py:67
  194.3 0.7 compare_reduce_fusion
  195.0 0.7 compare_reduce_fusion.2
  198.2 0.1 select_select_fusion
  198.4 10.4 %while.1 = (s32[]{:T(128)}, f32[512,512]{1,0:T(8,128)S(1)}, s32[4,2]{0,1:T(2,128)S(1)}, f32[4,128,128]{2,1,0:T(8,128)}, s32[]{:T(128)}) while((s32[]{:T(128)}, f32[512,512]{1,0:T(8,128)S(1)}, s32[4,2]{0,1:T(2,128)S(1)}, f32[4,128,128]{2,1,0:T(8,128)}, s32[]{:T(128)}) %tuple.39), condition=%wide.while_cond, body=%wide.while_body.sunk | while | flops 2 | bytes 132705 | solution.py:73
  198.4 0.1 constant_dynamic-slice_fusion.2
  198.5 0.5 fusion.73
  199.0 2.0 bitcast_dynamic-update-slice_fusion.2
  201.0 0.1 constant_dynamic-slice_fusion.2
  201.1 0.5 fusion.73
  201.6 2.0 bitcast_dynamic-update-slice_fusion.2
  203.7 0.5 fusion.73
  204.2 2.0 bitcast_dynamic-update-slice_fusion.2
  206.3 0.5 fusion.73
  206.8 2.0 bitcast_dynamic-update-slice_fusion.2
  208.8 40.1 %custom-call.34 = f32[4,128,128]{1,2,0:T(8,128)S(1)} custom-call(f32[4,128,128]{2,1,0:T(8,128)} %get-tuple-element.12), custom_call_target="InvertDiagBlocksLowerTriangular" | custom-call | tf_op jit(solution)/shard_map/jit(_solve_triangular)/triangular_solve | solution.py:73
  248.9 0.2 fusion.60
  249.1 0.3 convolution_subtract_fusion.3
  249.4 0.2 fusion.61
  249.6 0.4 convolution_subtract_fusion.2
  250.0 0.2 fusion.62
  250.2 0.5 convolution_subtract_fusion.4
  250.7 0.2 convolution_convert_fusion.1
  251.0 0.3 convolution_convert_fusion
  251.3 1.5 collective-permute-start.2
  252.8 3.2 %collective-permute-start.3 = (bf16[256,128]{1,0:T(8,128)(2,1)S(1)}, bf16[256,128]{1,0:T(8,128)(2,1)S(1)}, u32[]{:S(2)}, u32[]{:S(2)}) collective-permute-start(bf16[256,128]{1,0:T(8,128)(2,1)S(1)} %get-tuple-element.24), channel_id=1, source_target_pairs={{4,0},{8,4},{12,8},{16,12},{20,16},{24,20},{28,24},{0,28},{5,1},{9... | collective-permute-start | bytes 196616 | tf_op jit(solution)/shard_map/ppermute | solution.py:23
  256.0 0.1 iota_compare_fusion.4
  256.1 2.2 collective-permute-done.2
  258.4 0.1 collective-permute-done.3
  258.5 3.2 %gather_fusion = bf16[1024,128]{1,0:T(8,128)(2,1)S(1)} fusion(bf16[1024,128]{1,0:T(8,128)(2,1)S(1)} %pad_maximum_fusion, s32[1024]{0:T(1024)S(1)} %broadcast_clamp_fusion), kind=kCustom, calls=%fused_computation | custom fusion | bytes 528384 | tf_op jit(solution)/shard_map/jit(_take)/gather | solution.py:86
  261.7 0.2 copy.15
  261.9 1.1 fusion
  (40 shorter events, 0.6 us)
Async XLA Ops:
  6.5 255.4 %copy-start = (bf16[2,512,512]{2,1,0:T(8,128)(2,1)S(1)}, bf16[2,512,512]{2,1,0:T(8,128)(2,1)}, u32[]{:S(2)}) copy-start(bf16[2,512,512]{2,1,0:T(8,128)(2,1)} %param.15) | copy-start | bytes 3145732
  6.5 31.7 %copy-start.5 = (bf16[512,128]{1,0:T(8,128)(2,1)S(1)}, bf16[512,128]{1,0:T(8,128)(2,1)}, u32[]{:S(2)}) copy-start(bf16[512,128]{1,0:T(8,128)(2,1)} %param.8) | copy-start | bytes 393220
  6.5 83.9 %all-gather.6.cloned.1.call-start = ((), (), s32[]{:S(2)}) async-start(), calls=%async_computation.1 | async-start | bytes 2359296 | tf_op jit(solution)/shard_map/all_gather | solution.py:64
  7.7 18.7 %collective-permute-start = (bf16[64,128]{1,0:T(8,128)(2,1)S(1)}, bf16[64,128]{1,0:T(8,128)(2,1)S(1)}, u32[]{:S(2)}, u32[]{:S(2)}) collective-permute-start(bf16[64,128]{1,0:T(8,128)(2,1)S(1)} %get-tuple-element.25), channel_id=1, source_target_pairs={{0,4},{4,8},{8,12},{12,16},{16,20},{20,24},{24,28},{1,5},{5,9},{9,... | collective-permute-start | bytes 49160 | tf_op jit(solution)/shard_map/ppermute | solution.py:20
  12.6 13.8 %collective-permute-start.1 = (bf16[64,128]{1,0:T(8,128)(2,1)S(1)}, bf16[64,128]{1,0:T(8,128)(2,1)S(1)}, u32[]{:S(2)}, u32[]{:S(2)}) collective-permute-start(bf16[64,128]{1,0:T(8,128)(2,1)S(1)} %get-tuple-element.26), channel_id=1, source_target_pairs={{4,0},{8,4},{12,8},{16,12},{20,16},{24,20},{28,24},{5,1},{9,5},{13... | collective-permute-start | bytes 49160 | tf_op jit(solution)/shard_map/ppermute | solution.py:23
  37.4 0.8 copy-start.3
  38.2 54.9 %copy-start.6 = (s32[2,4]{1,0:T(2,128)S(1)}, s32[2,4]{1,0:T(2,128)}, u32[]{:S(2)}) copy-start(s32[2,4]{1,0:T(2,128)} %param.13) | copy-start | bytes 100
  39.3 69.1 %all-gather.4.cloned.1.call-start = ((), (), s32[]{:S(2)}) async-start(), calls=%async_computation | async-start | bytes 1310720 | tf_op jit(solution)/shard_map/all_gather | solution.py:66
  108.4 1.7 copy-start.1
  110.3 1.0 copy-start.2
  198.4 52.6 %copy-start.4 = (bf16[512,512]{1,0:T(8,128)(2,1)S(1)}, bf16[512,512]{1,0:T(8,128)(2,1)}, u32[]{:S(2)}) copy-start(bf16[512,512]{1,0:T(8,128)(2,1)} %copy-done.3) | copy-start | bytes 1572868
  198.4 57.7 %copy-start.7 = (s32[2]{0:T(128)S(1)}, s32[2]{0:T(128)}, u32[]{:S(2)}) copy-start(s32[2]{0:T(128)} %param.14) | copy-start | bytes 28
  251.3 7.1 %collective-permute-start.2 = (bf16[256,128]{1,0:T(8,128)(2,1)S(1)}, bf16[256,128]{1,0:T(8,128)(2,1)S(1)}, u32[]{:S(2)}, u32[]{:S(2)}) collective-permute-start(bf16[256,128]{1,0:T(8,128)(2,1)S(1)} %get-tuple-element.23), channel_id=1, source_target_pairs={{0,4},{4,8},{8,12},{12,16},{16,20},{20,24},{24,28},{28,0},{1,5},{5... | collective-permute-start | bytes 196616 | tf_op jit(solution)/shard_map/ppermute | solution.py:20
  252.8 5.7 %collective-permute-start.3 = (bf16[256,128]{1,0:T(8,128)(2,1)S(1)}, bf16[256,128]{1,0:T(8,128)(2,1)S(1)}, u32[]{:S(2)}, u32[]{:S(2)}) collective-permute-start(bf16[256,128]{1,0:T(8,128)(2,1)S(1)} %get-tuple-element.24), channel_id=1, source_target_pairs={{4,0},{8,4},{12,8},{16,12},{20,16},{24,20},{28,24},{0,28},{5,1},{9... | collective-permute-start | bytes 196616 | tf_op jit(solution)/shard_map/ppermute | solution.py:23
Sparse Core Ops, SparseCore 0:
  39.4 51.0 all-gather.5
  93.2 15.1 all-gather.3
